TPU v7x, 32 devices: a whole 2x2x4 slice. The times are simulated.
32 devices in a mesh: dp: 2 (over y), pipe: 4 (over x, core), seq: 4 (over z).
Axes of the slice: x: 2, y: 2, z: 4, core: 2. Of those that a mesh axis runs over, the one named last changes fastest.
Arguments:
- query_states: bfloat16 [8, 512, 8192], P(('dp', 'pipe'), 'seq'), parts along dimension 0, may hold values from -15 to 15
- projected_keys: bfloat16 [8, 512, 1024], P(('dp', 'pipe'), 'seq'), parts along dimension 0, may hold values from -8 to 8
- projected_values: bfloat16 [8, 512, 1024], P(('dp', 'pipe'), 'seq'), parts along dimension 0, may hold values from -6 to 6
- positions: int32 [8, 512], P(('dp', 'pipe'), 'seq'), parts along dimension 0, may hold values from 0 to 1023, as said below
- segments: int32 [8, 512], P(('dp', 'pipe'), 'seq'), parts along dimension 0, may hold values from 0 to 3, as said below
Outputs:
- handed: bfloat16 [8, 512, 8192], P(('dp', 'pipe'), 'seq'), parts along dimension 0
There are 2 independent parts, one for each index of `dp`. A program takes and returns all parts, laid end to end along the dimension named above; each array names one. Nothing has to cross between parts.
Inputs may be any that keep to these rules, and one draw needn't show every extreme that they name: `segments`: within each micro-batch ids never fall along the sequence, start at 0, every id occurs, and every document holds 4 or more tokens. `positions`: within a document a position is one more than the previous token's; the first document of each micro-batch starts at 0, and the last token of each micro-batch has position 1023.
All inputs are finite; a program needn't handle non-finite values.
Results may differ from a plain program's by a relative error of at most 0.0014.
The roundings to bfloat16 on the way count: a program that leaves them out, or rounds other values in their place, can miss the bound.
Values may be sent and summed in bfloat16 or wider, within the bound.
No kernel may reach another device: no remote copies, remote signals or barrier semaphores. Data moves between devices by JAX's collectives and lax.ppermute only.
A program may use at most 64 MiB of HBM per device.

v0:
```python
import math
import jax
import jax.numpy as jnp
from jax import lax
from jax.sharding import PartitionSpec as P

QUERY_HEADS = 64
KEY_VALUE_HEADS = 8
HEAD_SIZE = 128
rope_theta = 1000000.0
yarn_factor = 4.0
trained_length = 32768.0
fast_beta = 32.0
slow_beta = 1.0
masked_score = -1e30


def passed_along(block, axis, distance):
    devices = range(lax.axis_size(axis))
    route = [((i - distance) % len(devices), i) for i in devices]
    return lax.ppermute(block, axis, route)


def yarn_tables(positions, head_dim):
    half_dim = head_dim // 2
    pair_index = jnp.arange(half_dim, dtype=jnp.float32)
    base_freq = 1.0 / rope_theta ** (2.0 * pair_index / head_dim)
    lower = math.floor(
        head_dim
        * math.log(trained_length / (fast_beta * 2.0 * math.pi))
        / (2.0 * math.log(rope_theta))
    )
    upper = math.ceil(
        head_dim
        * math.log(trained_length / (slow_beta * 2.0 * math.pi))
        / (2.0 * math.log(rope_theta))
    )
    lower = max(lower, 0)
    upper = min(upper, head_dim - 1)
    upper = max(upper, lower + 1)
    ramp_value = jnp.clip((pair_index - lower) / (upper - lower), 0.0, 1.0)
    keep_share = 1.0 - ramp_value
    inv_freq = base_freq / yarn_factor * (1.0 - keep_share) + base_freq * keep_share
    attn_gain = 0.1 * math.log(yarn_factor) + 1.0
    angles = positions.astype(jnp.float32)[..., None] * inv_freq
    return (jnp.cos(angles) * attn_gain, jnp.sin(angles) * attn_gain)


def apply_rotation(states, cosine_table, sine_table):
    half_dim = states.shape[-1] // 2
    first_half = states[..., :half_dim]
    second_half = states[..., half_dim:]
    return jnp.concatenate(
        [
            first_half * cosine_table - second_half * sine_table,
            second_half * cosine_table + first_half * sine_table,
        ],
        axis=-1,
    )


def empty_running(query_rows, kv_count, group_count):
    return (
        jnp.full((query_rows, kv_count, group_count), masked_score, jnp.float32),
        jnp.zeros((query_rows, kv_count, group_count), jnp.float32),
        jnp.zeros((query_rows, kv_count, group_count, HEAD_SIZE), jnp.float32),
    )


def online_update(running, query_block, key_block, value_block, visible):
    best, denom, accum = running
    scores = jnp.einsum(
        "qkgd,nkd->qkgn", query_block, key_block, preferred_element_type=jnp.float32
    ) / math.sqrt(HEAD_SIZE)
    shown = visible[:, None, None, :]
    scores = jnp.where(shown, scores, masked_score)
    best_next = jnp.maximum(best, jnp.max(scores, axis=-1))
    weights = jnp.where(shown, jnp.exp(scores - best_next[..., None]), 0.0)
    rescale = jnp.exp(best - best_next)
    denom = denom * rescale + jnp.sum(weights, axis=-1)
    accum = accum * rescale[..., None] + jnp.einsum(
        "qkgn,nkd->qkgd",
        weights.astype(jnp.bfloat16),
        value_block,
        preferred_element_type=jnp.float32,
    )
    return (best_next, denom, accum)


def finish_running(running):
    best, denom, accum = running
    result = accum / denom[..., None]
    return result.reshape(result.shape[0], -1).astype(jnp.bfloat16)


def attend_local(grouped_queries, key_heads, value_head_rows, segment_ids):
    sequence_total = grouped_queries.shape[0]
    kv_count = grouped_queries.shape[1]
    group_count = grouped_queries.shape[2]
    block = min(512, sequence_total)
    block_count = sequence_total // block

    def one_block(block_index, finished):
        first_row = block_index * block
        query_block = lax.dynamic_slice_in_dim(grouped_queries, first_row, block, 0)
        query_segs = lax.dynamic_slice_in_dim(segment_ids, first_row, block, 0)
        query_ids = first_row + jnp.arange(block, dtype=jnp.int32)

        def key_step(key_index, running):
            first_key = key_index * block
            key_block = lax.dynamic_slice_in_dim(key_heads, first_key, block, 0)
            value_block = lax.dynamic_slice_in_dim(value_head_rows, first_key, block, 0)
            key_segs = lax.dynamic_slice_in_dim(segment_ids, first_key, block, 0)
            key_ids = first_key + jnp.arange(block, dtype=jnp.int32)
            visible = (key_ids[None, :] <= query_ids[:, None]) & (
                key_segs[None, :] == query_segs[:, None]
            )
            return online_update(running, query_block, key_block, value_block, visible)

        running = lax.fori_loop(
            0, block_index + 1, key_step, empty_running(block, kv_count, group_count)
        )
        return lax.dynamic_update_slice_in_dim(finished, finish_running(running), first_row, 0)

    finished = jnp.zeros((sequence_total, kv_count * group_count * HEAD_SIZE), jnp.bfloat16)
    return lax.fori_loop(0, block_count, one_block, finished)


def on_device(query_states, projected_keys, projected_values, positions, segments):
    token_rows = query_states.shape[1]
    cosine_table, sine_table = yarn_tables(positions[0], HEAD_SIZE)
    cosine_table = cosine_table[:, None, :]
    sine_table = sine_table[:, None, :]
    rotated_queries = apply_rotation(
        query_states[0].astype(jnp.float32).reshape(token_rows, QUERY_HEADS, HEAD_SIZE),
        cosine_table,
        sine_table,
    ).astype(jnp.bfloat16)
    rotated_keys = apply_rotation(
        projected_keys[0].astype(jnp.float32).reshape(token_rows, KEY_VALUE_HEADS, HEAD_SIZE),
        cosine_table,
        sine_table,
    ).astype(jnp.bfloat16)
    value_head_rows = projected_values[0].reshape(token_rows, KEY_VALUE_HEADS, HEAD_SIZE)
    segment_ids = segments[0]
    row_width = lax.axis_size("seq")
    per_device = QUERY_HEADS // row_width
    key_value_local = max(1, KEY_VALUE_HEADS // row_width)
    repeat_count = max(1, row_width // KEY_VALUE_HEADS)
    query_send = rotated_queries.reshape(token_rows, row_width, per_device * HEAD_SIZE)
    key_send = jnp.broadcast_to(
        rotated_keys.reshape(
            token_rows, KEY_VALUE_HEADS // key_value_local, 1, key_value_local * HEAD_SIZE
        ),
        (token_rows, KEY_VALUE_HEADS // key_value_local, repeat_count, key_value_local * HEAD_SIZE),
    ).reshape(token_rows, row_width, key_value_local * HEAD_SIZE)
    value_send = jnp.broadcast_to(
        value_head_rows.reshape(
            token_rows, KEY_VALUE_HEADS // key_value_local, 1, key_value_local * HEAD_SIZE
        ),
        (token_rows, KEY_VALUE_HEADS // key_value_local, repeat_count, key_value_local * HEAD_SIZE),
    ).reshape(token_rows, row_width, key_value_local * HEAD_SIZE)
    segment_send = jnp.broadcast_to(
        segment_ids.astype(jnp.bfloat16)[:, None, None], (token_rows, row_width, 1)
    )
    query_all, key_all, value_all, segment_all = (
        lax.all_to_all(query_send, "seq", split_axis=1, concat_axis=0, tiled=True),
        lax.all_to_all(key_send, "seq", split_axis=1, concat_axis=0, tiled=True),
        lax.all_to_all(value_send, "seq", split_axis=1, concat_axis=0, tiled=True),
        lax.all_to_all(segment_send, "seq", split_axis=1, concat_axis=0, tiled=True),
    )
    sequence_total = token_rows * row_width
    heads_out = attend_local(
        query_all.reshape(
            sequence_total, key_value_local, per_device // key_value_local, HEAD_SIZE
        ),
        key_all.reshape(sequence_total, key_value_local, HEAD_SIZE),
        value_all.reshape(sequence_total, key_value_local, HEAD_SIZE),
        segment_all.reshape(sequence_total).astype(jnp.int32),
    )
    rows_out = lax.all_to_all(
        heads_out.reshape(sequence_total, 1, per_device * HEAD_SIZE),
        "seq",
        split_axis=0,
        concat_axis=1,
        tiled=True,
    )
    rows_out = rows_out.reshape(token_rows, QUERY_HEADS * HEAD_SIZE)
    rows_out = passed_along(rows_out, "pipe", 1)
    return rows_out[None]


def solution(mesh):
    placed = (
        P(("dp", "pipe"), "seq", None),
        P(("dp", "pipe"), "seq", None),
        P(("dp", "pipe"), "seq", None),
        P(("dp", "pipe"), "seq"),
        P(("dp", "pipe"), "seq"),
    )
    return jax.shard_map(
        on_device,
        mesh=mesh,
        in_specs=placed,
        out_specs=P(("dp", "pipe"), "seq", None),
        check_vma=False,
    )
```

profile of v0, /device:TPU:0, one launch (start us, length us, event | category | flops | bytes accessed | tf_op | source)
XLA Modules:
  0.0 201.0 jit_solution(10546775687055647915)
XLA Ops:
  0.0 0.0 copy-start
  0.0 0.8 convert_bitcast_fusion.1
  0.8 0.6 broadcast_in_dim.51
  1.4 6.3 %all-to-all-start = ((bf16[128,4,1]{0,2,1:T(2,128)(2,1)}), bf16[128,4,1]{0,2,1:T(2,128)(2,1)S(1)}, u32[]{:S(2)}, u32[]{:S(2)}) async-start(bf16[128,4,1]{0,2,1:T(2,128)(2,1)} %broadcast_in_dim.51), calls=%async_computation | async-start | bytes 4096 | tf_op jit(solution)/shard_map/all_to_all | solution.py:170
  7.8 0.7 convert_bitcast_fusion
  8.4 1.1 copy.44
  9.5 0.0 copy-start.1
  9.5 0.2 fusion.15
  9.7 0.1 subtract_convert_fusion.1
  9.8 0.7 pad_maximum_fusion.1
  10.5 2.8 %all-to-all-done = bf16[128,4,1]{0,2,1:T(2,128)(2,1)S(1)} async-done(((bf16[128,4,1]{0,2,1:T(2,128)(2,1)}), bf16[128,4,1]{0,2,1:T(2,128)(2,1)S(1)}, u32[]{:S(2)}, u32[]{:S(2)}) %all-to-all-start) | async-done | bytes 1056 | tf_op jit(solution)/shard_map/all_to_all | solution.py:170
  13.3 3.4 %all-to-all-start.1 = ((bf16[128,4,256]{0,2,1:T(8,128)(2,1)}), bf16[128,4,256]{0,2,1:T(8,128)(2,1)S(1)}, u32[]{:S(2)}, u32[]{:S(2)}) async-start(bf16[128,4,256]{0,2,1:T(8,128)(2,1)} %bitcast.8), calls=%async_computation.1 | async-start | bytes 524288 | tf_op jit(solution)/shard_map/all_to_all | solution.py:168
  16.7 0.0 copy-done
  16.7 2.9 %copy.46 = f32[1,128,8192]{1,2,0:T(8,128)} copy(bf16[1,128,8192]{2,1,0:T(8,128)(2,1)S(1)} %copy-done) | data formatting | bytes 6291456 | tf_op jit(solution)/shard_map/convert_element_type | solution.py:135
  19.7 0.0 copy-done.1
  19.7 0.8 copy.50
  20.5 3.3 %all-to-all-done.1 = bf16[128,4,256]{0,2,1:T(8,128)(2,1)S(1)} async-done(((bf16[128,4,256]{0,2,1:T(8,128)(2,1)}), bf16[128,4,256]{0,2,1:T(8,128)(2,1)S(1)}, u32[]{:S(2)}, u32[]{:S(2)}) %all-to-all-start.1) | async-done | bytes 262176 | tf_op jit(solution)/shard_map/all_to_all | solution.py:168
  23.8 3.4 %all-to-all-start.3 = ((bf16[128,4,256]{0,2,1:T(8,128)(2,1)}), bf16[128,4,256]{0,2,1:T(8,128)(2,1)S(1)}, u32[]{:S(2)}, u32[]{:S(2)}) async-start(bf16[128,4,256]{0,2,1:T(8,128)(2,1)} %bitcast.17), calls=%async_computation.3 | async-start | bytes 524288 | tf_op jit(solution)/shard_map/all_to_all | solution.py:169
  27.2 2.8 %subtract_convert_fusion = (bf16[128,64,64]{0,2,1:T(8,128)(2,1)S(1)}, bf16[128,64,64]{0,2,1:T(8,128)(2,1)S(1)}) fusion(f32[128,64,128]{0,2,1:T(8,128)} %bitcast.64, f32[128,64]{0,1:T(8,128)S(1)} %get-tuple-element.110, f32[128,64]{0,1:T(8,128)S(1)} %get-tuple-element.109), kind=kLoop, calls=%fused_computation.14 | loop fusion | flops 4194304 | bytes 6356992 | tf_op jit(solution)/shard_map/convert.5
  30.0 1.5 pad_maximum_fusion
  31.6 2.4 %all-to-all-done.3 = bf16[128,4,256]{0,2,1:T(8,128)(2,1)S(1)} async-done(((bf16[128,4,256]{0,2,1:T(8,128)(2,1)}), bf16[128,4,256]{0,2,1:T(8,128)(2,1)S(1)}, u32[]{:S(2)}, u32[]{:S(2)}) %all-to-all-start.3) | async-done | bytes 262176 | tf_op jit(solution)/shard_map/all_to_all | solution.py:169
  33.9 3.6 %all-to-all-start.2 = ((bf16[128,4,2048]{0,2,1:T(8,128)(2,1)}), bf16[128,4,2048]{0,2,1:T(8,128)(2,1)S(1)}, u32[]{:S(2)}, u32[]{:S(2)}) async-start(bf16[128,4,2048]{0,2,1:T(8,128)(2,1)} %bitcast.13), calls=%async_computation.2 | async-start | bytes 4194304 | tf_op jit(solution)/shard_map/all_to_all | solution.py:167
  37.6 0.2 fusion.12
  37.8 0.1 copy.45
  37.9 0.1 reshape.183
  38.0 0.2 copy.51
  38.2 0.1 reshape.192
  38.3 43.6 %all-to-all-done.2 = bf16[128,4,2048]{0,2,1:T(8,128)(2,1)S(1)} async-done(((bf16[128,4,2048]{0,2,1:T(8,128)(2,1)}), bf16[128,4,2048]{0,2,1:T(8,128)(2,1)S(1)}, u32[]{:S(2)}, u32[]{:S(2)}) %all-to-all-start.2) | async-done | bytes 2097184 | tf_op jit(solution)/shard_map/all_to_all | solution.py:167
  82.0 2.6 %copy.47 = bf16[4,128,1,2048]{3,1,0,2:T(8,128)(2,1)} copy(bf16[4,128,1,2048]{1,3,0,2:T(8,128)(2,1)S(1)} %bitcast.67) | data formatting | bytes 4194304 | tf_op jit(solution)/shard_map/all_to_all | solution.py:167
  84.6 2.2 %copy.62 = bf16[64,8,16,128]{3,2,1,0:T(8,128)(2,1)S(1)} copy(bf16[64,8,16,128]{3,1,2,0:T(8,128)(2,1)} %bitcast.68) | data formatting | bytes 4194304
  86.8 3.8 %fusion = (f32[512,2,8]{0,2,1:T(8,128)S(1)}, f32[2,512,512,8]{2,1,3,0:T(8,128)S(1)}) fusion(pred[512,512]{0,1:T(8,128)(4,1)S(1)} %fusion.12, bf16[512,2,8,128]{3,2,1,0:T(8,128)(2,1)S(1)} %bitcast.65, bf16[512,2,128,1]{2,1,0,3:T(2,128)(2,1)S(1)} %bitcast.73), kind=kOutput, calls=%fused_computation.2 | convolution fusion | flops 1086316544 | bytes 19431424 | tf_op jit(solution)/shard_map/while/body/eval_jaxpr/while/body/qkgd,nkd->qkgn/dot_general | solution.py:72
  90.6 4.0 %fusion.1 = f32[512,2,8]{0,2,1:T(8,128)S(1)} fusion(f32[2,512,512,8]{2,1,3,0:T(8,128)S(1)} %get-tuple-element.112, f32[512,2,8]{0,2,1:T(8,128)S(1)} %broadcast_maximum_fusion, pred[512,512]{0,1:T(8,128)(4,1)S(1)} %fusion.12), kind=kLoop, calls=%fused_computation.3 | loop fusion | flops 20963328 | bytes 17104896 | tf_op jit(solution)/shard_map/while/body/eval_jaxpr/while/body/reduce_sum | solution.py:80
  94.6 6.0 %fusion.7 = bf16[512,2,8,128]{0,3,2,1:T(8,128)(2,1)} fusion(f32[2,512,512,8]{2,1,3,0:T(8,128)S(1)} %get-tuple-element.112, f32[512,2,8]{0,2,1:T(8,128)S(1)} %broadcast_maximum_fusion, pred[512,512]{0,1:T(8,128)(4,1)S(1)} %fusion.12, f32[512,2,8]{0,2,1:T(8,128)S(1)} %get-tuple-element.108, f32[512,2,8]{0,2,1:T(8,128)S(1)} %get-tuple-element.107, ...), kind=kOutput, calls=%fused_computation.9 | convolution fusion | flops 1097859072 | bytes 19496960 | tf_op jit(solution)/shard_map/while/body/eval_jaxpr/while/body/qkgn,nkd->qkgd/dot_general | solution.py:81
  100.7 0.5 broadcast.185
  101.2 3.8 %reduce = bf16[512,2048]{0,1:T(8,128)(2,1)S(1)} reduce(bf16[512,1,2048]{0,2,1:T(8,128)(2,1)} %bitcast.69, bf16[]{:T(256)} %broadcast.185), dimensions={1}, to_apply=%copy.53.reduce_sub_computation | reduce | bytes 4194306 | tf_op jit(solution)/shard_map/while/body/eval_jaxpr/convert_element_type | solution.py:93
  105.0 2.4 %copy.71 = bf16[512,2048]{1,0:T(8,128)(2,1)} copy(bf16[512,2048]{0,1:T(8,128)(2,1)S(1)} %reduce) | data formatting | bytes 4194304
  107.4 4.5 %reshape.194 = bf16[4,2,131072]{2,1,0:T(2,128)(2,1)} reshape(bf16[512,2048]{1,0:T(8,128)(2,1)} %copy.71) | data formatting | bytes 4194304
  111.9 51.3 %all_to_all.69 = bf16[4,2,131072]{2,1,0:T(2,128)(2,1)S(1)} all-to-all(bf16[4,2,131072]{2,1,0:T(2,128)(2,1)} %reshape.194), channel_id=1, replica_groups=mesh['dp'=2,'pipe'=4,'seq'=4] {'seq'}, dimensions={0} | all-to-all | bytes 4194304 | tf_op jit(solution)/shard_map/all_to_all | solution.py:181
  163.2 3.4 %reshape.195 = bf16[512,1,2048]{2,1,0:T(2,128)(2,1)} reshape(bf16[4,2,131072]{2,1,0:T(2,128)(2,1)S(1)} %all_to_all.69) | data formatting | bytes 4194304
  166.5 3.5 %copy.61 = bf16[512,1,2048]{2,0,1:T(8,128)(2,1)S(1)} copy(bf16[512,1,2048]{2,1,0:T(2,128)(2,1)} %reshape.195) | data formatting | bytes 4194304
  170.0 2.5 %copy.54 = bf16[128,4,1,2048]{0,3,1,2:T(8,128)(2,1)} copy(bf16[128,4,1,2048]{3,0,1,2:T(8,128)(2,1)S(1)} %bitcast.66) | data formatting | bytes 4194304 | tf_op jit(solution)/shard_map/all_to_all | solution.py:181
  172.5 0.0 collective-permute-start
  172.5 25.7 %collective-permute-done = bf16[128,8192]{0,1:T(8,128)(2,1)S(1)} collective-permute-done((bf16[128,8192]{0,1:T(8,128)(2,1)}, bf16[128,8192]{0,1:T(8,128)(2,1)S(1)}, u32[]{:S(2)}, u32[]{:S(2)}) %collective-permute-start) | collective-permute-done | bytes 2097184 | tf_op jit(solution)/shard_map/ppermute | solution.py:21
  198.2 2.9 %copy.55 = bf16[1,128,8192]{2,1,0:T(8,128)(2,1)} copy(bf16[1,128,8192]{1,2,0:T(8,128)(2,1)S(1)} %bitcast.71) | data formatting | bytes 4194304 | tf_op jit(solution)/shard_map/broadcast_in_dim | solution.py:190
  (4 shorter events, 0.0 us)
Async XLA Ops:
  0.0 16.7 %copy-start = (bf16[1,128,8192]{2,1,0:T(8,128)(2,1)S(1)}, bf16[1,128,8192]{2,1,0:T(8,128)(2,1)}, u32[]{:S(2)}) copy-start(bf16[1,128,8192]{2,1,0:T(8,128)(2,1)} %param.5) | copy-start | bytes 6291460
  1.4 11.9 %all-to-all-start = ((bf16[128,4,1]{0,2,1:T(2,128)(2,1)}), bf16[128,4,1]{0,2,1:T(2,128)(2,1)S(1)}, u32[]{:S(2)}, u32[]{:S(2)}) async-start(bf16[128,4,1]{0,2,1:T(2,128)(2,1)} %broadcast_in_dim.51), calls=%async_computation | async-start | bytes 4096 | tf_op jit(solution)/shard_map/all_to_all | solution.py:170
  9.5 10.2 %copy-start.1 = (bf16[1,128,1024]{2,1,0:T(8,128)(2,1)S(1)}, bf16[1,128,1024]{2,1,0:T(8,128)(2,1)}, u32[]{:S(2)}) copy-start(bf16[1,128,1024]{2,1,0:T(8,128)(2,1)} %param.7) | copy-start | bytes 786436
  13.3 10.5 %all-to-all-start.1 = ((bf16[128,4,256]{0,2,1:T(8,128)(2,1)}), bf16[128,4,256]{0,2,1:T(8,128)(2,1)S(1)}, u32[]{:S(2)}, u32[]{:S(2)}) async-start(bf16[128,4,256]{0,2,1:T(8,128)(2,1)} %bitcast.8), calls=%async_computation.1 | async-start | bytes 524288 | tf_op jit(solution)/shard_map/all_to_all | solution.py:168
  23.8 10.2 %all-to-all-start.3 = ((bf16[128,4,256]{0,2,1:T(8,128)(2,1)}), bf16[128,4,256]{0,2,1:T(8,128)(2,1)S(1)}, u32[]{:S(2)}, u32[]{:S(2)}) async-start(bf16[128,4,256]{0,2,1:T(8,128)(2,1)} %bitcast.17), calls=%async_computation.3 | async-start | bytes 524288 | tf_op jit(solution)/shard_map/all_to_all | solution.py:169
  33.9 48.0 %all-to-all-start.2 = ((bf16[128,4,2048]{0,2,1:T(8,128)(2,1)}), bf16[128,4,2048]{0,2,1:T(8,128)(2,1)S(1)}, u32[]{:S(2)}, u32[]{:S(2)}) async-start(bf16[128,4,2048]{0,2,1:T(8,128)(2,1)} %bitcast.13), calls=%async_computation.2 | async-start | bytes 4194304 | tf_op jit(solution)/shard_map/all_to_all | solution.py:167
  172.5 25.7 %collective-permute-start = (bf16[128,8192]{0,1:T(8,128)(2,1)}, bf16[128,8192]{0,1:T(8,128)(2,1)S(1)}, u32[]{:S(2)}, u32[]{:S(2)}) collective-permute-start(bf16[128,8192]{0,1:T(8,128)(2,1)} %bitcast.70), channel_id=1, source_target_pairs={{12,0},{0,4},{4,8},{8,12},{13,1},{1,5},{5,9},{9,13},{14,2},{2,6},{... | collective-permute-start | bytes 6291464 | tf_op jit(solution)/shard_map/ppermute | solution.py:21
where the time goes:
time: 202 us; the launch traced here: 201 us
  waiting for transfers between devices  77.8 us (39%)
  blocking collectives  51.3 us (25%)
  local copies, waits for them, and re-layouts  30.3 us (15%)
  starting transfers between devices  16.8 us (8%)
  other arithmetic  14.9 us (7%)
  matrix products  9.84 us (5%)
    all_to_all x1, blocking collectives, on_device(): lax.all_to_all(heads_out.reshape(sequence_total, 1, per_device * HEAD_SIZ...  51.3 us
    all_to_all x1, waiting for transfers between devices, on_device(): lax.all_to_all(query_send, 'seq', split_axis=1, concat_axis=0, tiled=True)  43.6 us
    ppermute x1, waiting for transfers between devices, passed_along(): return lax.ppermute(block, axis, route)  25.7 us
    unnamed x10, local copies, waits for them, and re-layouts  16.7 us
    all_to_all x1, starting transfers between devices, on_device(): lax.all_to_all(segment_send, 'seq', split_axis=1, concat_axis=0, tiled=True)  6.35 us
    dot_general x1, matrix products, online_update(): jnp.einsum('qkgn,nkd->qkgd', weights.astype(jnp.bfloat16), value_block, p...  6.04 us
  transfers between devices with their start and end apart: 5, of which 5 were waited for; matrix products, arithmetic and copies ran while one was open for 6% of the time, Pallas kernels for 0%

commit v1 on v0

--- a/solution.py
+++ b/solution.py
@@ -164,7 +164,12 @@
         segment_ids.astype(jnp.bfloat16)[:, None, None], (token_rows, row_width, 1)
     )
     query_all, key_all, value_all, segment_all = (
-        lax.all_to_all(query_send, "seq", split_axis=1, concat_axis=0, tiled=True),
+        jnp.concatenate(
+            lax.all_to_all(
+                jnp.stack(jnp.split(query_send, lax.axis_size("seq"), axis=1)), "seq", 0, 0
+            ),
+            axis=0,
+        ),
         lax.all_to_all(key_send, "seq", split_axis=1, concat_axis=0, tiled=True),
         lax.all_to_all(value_send, "seq", split_axis=1, concat_axis=0, tiled=True),
         lax.all_to_all(segment_send, "seq", split_axis=1, concat_axis=0, tiled=True),

time: 202 us -> 208 us (1.030)
  waiting for transfers between devices: 77.8 us -> 80.6 us
    all_to_all x1, waiting for transfers between devices: 2.38 us -> 5.2 us  [on_device(): lax.all_to_all(value_send, 'seq', split_axis=1, concat_axis=0, tiled=True)]
    all_to_all x1, waiting for transfers between devices: 2.79 us -> 0.01 us  [on_device(): lax.all_to_all(segment_send, 'seq', split_axis=1, concat_axis=0, tiled=True)]
    another operation x2 -> x3, other arithmetic: 2.92 us -> 4.49 us
    unnamed x10 -> x8, local copies, waits for them, and re-layouts: 16.7 us -> 16.7 us
  transfers between devices with their start and end apart: 5 -> 5, of which waited for: 5 -> 4; matrix products, arithmetic and copies ran while one was open for 6% -> 6% of each run, Pallas kernels for 0% -> 0%
where the time goes in v1:
time: 208 us; the launch traced here: 207 us
  waiting for transfers between devices  80.6 us (39%)
  blocking collectives  51.3 us (25%)
  local copies, waits for them, and re-layouts  31.9 us (15%)
  starting transfers between devices  18.6 us (9%)
  other arithmetic  15 us (7%)
  matrix products  9.85 us (5%)
    all_to_all x1, blocking collectives, on_device(): lax.all_to_all(heads_out.reshape(sequence_total, 1, per_device * HEAD_SIZ...  51.3 us
    all_to_all x1, waiting for transfers between devices, on_device(): lax.all_to_all(jnp.stack(jnp.split(query_send, lax.axis_size('seq'), axis...  44.5 us
    ppermute x1, waiting for transfers between devices, passed_along(): return lax.ppermute(block, axis, route)  25.7 us
    unnamed x8, local copies, waits for them, and re-layouts  16.7 us
    all_to_all x1, starting transfers between devices, on_device(): lax.all_to_all(segment_send, 'seq', split_axis=1, concat_axis=0, tiled=True)  6.35 us
    dot_general x1, matrix products, online_update(): jnp.einsum('qkgn,nkd->qkgd', weights.astype(jnp.bfloat16), value_block, p...  6.04 us
    all_to_all x1, waiting for transfers between devices, on_device(): lax.all_to_all(key_send, 'seq', split_axis=1, concat_axis=0, tiled=True)  5.28 us
    all_to_all x1, waiting for transfers between devices, on_device(): lax.all_to_all(value_send, 'seq', split_axis=1, concat_axis=0, tiled=True)  5.2 us
  transfers between devices with their start and end apart: 5, of which 4 were waited for; matrix products, arithmetic and copies ran while one was open for 6% of the time, Pallas kernels for 0%

profile of v1, /device:TPU:0, one launch (start us, length us, event | category | flops | bytes accessed | tf_op | source)
XLA Modules:
  0.0 207.4 jit_solution(5358513350038586653)
XLA Ops:
  0.0 0.7 convert_bitcast_fusion.1
  0.7 0.6 broadcast_in_dim.51
  1.3 6.3 %all-to-all-start = ((bf16[128,4,1]{0,2,1:T(2,128)(2,1)}), bf16[128,4,1]{0,2,1:T(2,128)(2,1)S(1)}, u32[]{:S(2)}, u32[]{:S(2)}) async-start(bf16[128,4,1]{0,2,1:T(2,128)(2,1)} %broadcast_in_dim.51), calls=%async_computation | async-start | bytes 4096 | tf_op jit(solution)/shard_map/all_to_all | solution.py:175
  7.6 0.7 convert_bitcast_fusion
  8.3 0.0 copy-start
  8.3 1.1 copy.53
  9.4 0.2 fusion.15
  9.6 0.1 subtract_convert_fusion.1
  9.7 0.7 pad_maximum_fusion.2
  10.4 4.3 %copy.55 = f32[1,128,8192]{1,2,0:T(8,128)} copy(bf16[1,128,8192]{2,1,0:T(8,128)(2,1)} %param.5) | data formatting | bytes 6291456 | tf_op jit(solution)/shard_map/convert_element_type | solution.py:135
  14.7 0.0 copy-done
  14.7 0.8 copy.61
  15.6 0.0 all-to-all-done
  15.6 5.1 %all-to-all-start.1 = ((bf16[128,4,256]{0,2,1:T(8,128)(2,1)}), bf16[128,4,256]{0,2,1:T(8,128)(2,1)S(1)}, u32[]{:S(2)}, u32[]{:S(2)}) async-start(bf16[128,4,256]{0,2,1:T(8,128)(2,1)} %bitcast.8), calls=%async_computation.1 | async-start | bytes 524288 | tf_op jit(solution)/shard_map/all_to_all | solution.py:173
  20.7 2.8 %subtract_convert_fusion = (bf16[128,64,64]{0,2,1:T(8,128)(2,1)S(1)}, bf16[128,64,64]{0,2,1:T(8,128)(2,1)S(1)}) fusion(f32[128,64,128]{0,2,1:T(8,128)} %bitcast.69, f32[128,64]{0,1:T(8,128)S(1)} %get-tuple-element.114, f32[128,64]{0,1:T(8,128)S(1)} %get-tuple-element.113), kind=kLoop, calls=%fused_computation.15 | loop fusion | flops 4194304 | bytes 6356992 | tf_op jit(solution)/shard_map/convert.5
  23.5 0.2 pad_maximum_fusion
  23.7 5.3 %all-to-all-done.1 = bf16[128,4,256]{0,2,1:T(8,128)(2,1)S(1)} async-done(((bf16[128,4,256]{0,2,1:T(8,128)(2,1)}), bf16[128,4,256]{0,2,1:T(8,128)(2,1)S(1)}, u32[]{:S(2)}, u32[]{:S(2)}) %all-to-all-start.1) | async-done | bytes 262176 | tf_op jit(solution)/shard_map/all_to_all | solution.py:173
  29.0 3.4 %all-to-all-start.3 = ((bf16[128,4,256]{0,2,1:T(8,128)(2,1)}), bf16[128,4,256]{0,2,1:T(8,128)(2,1)S(1)}, u32[]{:S(2)}, u32[]{:S(2)}) async-start(bf16[128,4,256]{0,2,1:T(8,128)(2,1)} %bitcast.19), calls=%async_computation.3 | async-start | bytes 524288 | tf_op jit(solution)/shard_map/all_to_all | solution.py:174
  32.4 0.1 slice_bitcast_fusion.3
  32.5 1.6 pad_maximum_fusion.1
  34.1 5.2 %all-to-all-done.3 = bf16[128,4,256]{0,2,1:T(8,128)(2,1)S(1)} async-done(((bf16[128,4,256]{0,2,1:T(8,128)(2,1)}), bf16[128,4,256]{0,2,1:T(8,128)(2,1)S(1)}, u32[]{:S(2)}, u32[]{:S(2)}) %all-to-all-start.3) | async-done | bytes 262176 | tf_op jit(solution)/shard_map/all_to_all | solution.py:174
  39.3 3.8 %all-to-all-start.2 = ((bf16[4,128,1,2048]{1,3,2,0:T(8,128)(2,1)}), bf16[4,128,1,2048]{1,3,2,0:T(8,128)(2,1)S(1)}, u32[]{:S(2)}, u32[]{:S(2)}) async-start(bf16[4,128,1,2048]{1,3,2,0:T(8,128)(2,1)} %pad_maximum_fusion.1), calls=%async_computation.2 | async-start | bytes 4194304 | tf_op jit(solution)/shard_map/all_to_all | solution.py:168
  43.1 0.2 fusion.12
  43.3 0.1 copy.54
  43.5 0.1 reshape.179
  43.6 0.2 copy.62
  43.8 0.1 reshape.187
  43.9 44.5 %all-to-all-done.2 = bf16[4,128,1,2048]{1,3,2,0:T(8,128)(2,1)S(1)} async-done(((bf16[4,128,1,2048]{1,3,2,0:T(8,128)(2,1)}), bf16[4,128,1,2048]{1,3,2,0:T(8,128)(2,1)S(1)}, u32[]{:S(2)}, u32[]{:S(2)}) %all-to-all-start.2) | async-done | bytes 2097184 | tf_op jit(solution)/shard_map/all_to_all | solution.py:168
  88.4 2.6 %copy.58 = bf16[4,128,1,2048]{3,1,0,2:T(8,128)(2,1)} copy(bf16[4,128,1,2048]{1,3,2,0:T(8,128)(2,1)S(1)} %all-to-all-done.2) | data formatting | bytes 4194304 | tf_op jit(solution)/shard_map/all_to_all | solution.py:168
  90.9 2.2 %copy.74 = bf16[64,8,16,128]{3,2,1,0:T(8,128)(2,1)S(1)} copy(bf16[64,8,16,128]{3,1,2,0:T(8,128)(2,1)} %bitcast.73) | data formatting | bytes 4194304
  93.2 3.8 %fusion = (f32[512,2,8]{0,2,1:T(8,128)S(1)}, f32[2,512,512,8]{2,1,3,0:T(8,128)S(1)}) fusion(pred[512,512]{0,1:T(8,128)(4,1)S(1)} %fusion.12, bf16[512,2,8,128]{3,2,1,0:T(8,128)(2,1)S(1)} %bitcast.70, bf16[512,2,128,1]{2,1,0,3:T(2,128)(2,1)S(1)} %bitcast.78), kind=kOutput, calls=%fused_computation.2 | convolution fusion | flops 1086316544 | bytes 19431424 | tf_op jit(solution)/shard_map/while/body/eval_jaxpr/while/body/qkgd,nkd->qkgn/dot_general | solution.py:72
  97.0 4.0 %fusion.1 = f32[512,2,8]{0,2,1:T(8,128)S(1)} fusion(f32[2,512,512,8]{2,1,3,0:T(8,128)S(1)} %get-tuple-element.116, f32[512,2,8]{0,2,1:T(8,128)S(1)} %broadcast_maximum_fusion, pred[512,512]{0,1:T(8,128)(4,1)S(1)} %fusion.12), kind=kLoop, calls=%fused_computation.3 | loop fusion | flops 20963328 | bytes 17104896 | tf_op jit(solution)/shard_map/while/body/eval_jaxpr/while/body/reduce_sum | solution.py:80
  101.0 6.0 %fusion.7 = bf16[512,2,8,128]{0,3,2,1:T(8,128)(2,1)} fusion(f32[2,512,512,8]{2,1,3,0:T(8,128)S(1)} %get-tuple-element.116, f32[512,2,8]{0,2,1:T(8,128)S(1)} %broadcast_maximum_fusion, pred[512,512]{0,1:T(8,128)(4,1)S(1)} %fusion.12, f32[512,2,8]{0,2,1:T(8,128)S(1)} %get-tuple-element.112, f32[512,2,8]{0,2,1:T(8,128)S(1)} %get-tuple-element.111, ...), kind=kOutput, calls=%fused_computation.9 | convolution fusion | flops 1097859072 | bytes 19496960 | tf_op jit(solution)/shard_map/while/body/eval_jaxpr/while/body/qkgn,nkd->qkgd/dot_general | solution.py:81
  107.1 0.5 broadcast.185
  107.6 3.8 %reduce = bf16[512,2048]{0,1:T(8,128)(2,1)S(1)} reduce(bf16[512,1,2048]{0,2,1:T(8,128)(2,1)} %bitcast.74, bf16[]{:T(256)} %broadcast.185), dimensions={1}, to_apply=%copy.64.reduce_sub_computation | reduce | bytes 4194306 | tf_op jit(solution)/shard_map/while/body/eval_jaxpr/convert_element_type | solution.py:93
  111.4 2.4 %copy.83 = bf16[512,2048]{1,0:T(8,128)(2,1)} copy(bf16[512,2048]{0,1:T(8,128)(2,1)S(1)} %reduce) | data formatting | bytes 4194304
  113.8 4.5 %reshape.189 = bf16[4,2,131072]{2,1,0:T(2,128)(2,1)} reshape(bf16[512,2048]{1,0:T(8,128)(2,1)} %copy.83) | data formatting | bytes 4194304
  118.2 51.3 %all_to_all.59 = bf16[4,2,131072]{2,1,0:T(2,128)(2,1)S(1)} all-to-all(bf16[4,2,131072]{2,1,0:T(2,128)(2,1)} %reshape.189), channel_id=1, replica_groups=mesh['dp'=2,'pipe'=4,'seq'=4] {'seq'}, dimensions={0} | all-to-all | bytes 4194304 | tf_op jit(solution)/shard_map/all_to_all | solution.py:186
  169.6 3.4 %reshape.190 = bf16[512,1,2048]{2,1,0:T(2,128)(2,1)} reshape(bf16[4,2,131072]{2,1,0:T(2,128)(2,1)S(1)} %all_to_all.59) | data formatting | bytes 4194304
  172.9 3.5 %copy.73 = bf16[512,1,2048]{2,0,1:T(8,128)(2,1)S(1)} copy(bf16[512,1,2048]{2,1,0:T(2,128)(2,1)} %reshape.190) | data formatting | bytes 4194304
  176.4 2.5 %copy.65 = bf16[128,4,1,2048]{0,3,1,2:T(8,128)(2,1)} copy(bf16[128,4,1,2048]{3,0,1,2:T(8,128)(2,1)S(1)} %bitcast.71) | data formatting | bytes 4194304 | tf_op jit(solution)/shard_map/all_to_all | solution.py:186
  178.9 0.0 collective-permute-start
  178.9 25.7 %collective-permute-done = bf16[128,8192]{0,1:T(8,128)(2,1)S(1)} collective-permute-done((bf16[128,8192]{0,1:T(8,128)(2,1)}, bf16[128,8192]{0,1:T(8,128)(2,1)S(1)}, u32[]{:S(2)}, u32[]{:S(2)}) %collective-permute-start) | collective-permute-done | bytes 2097184 | tf_op jit(solution)/shard_map/ppermute | solution.py:21
  204.5 2.9 %copy.66 = bf16[1,128,8192]{2,1,0:T(8,128)(2,1)} copy(bf16[1,128,8192]{1,2,0:T(8,128)(2,1)S(1)} %bitcast.76) | data formatting | bytes 4194304 | tf_op jit(solution)/shard_map/broadcast_in_dim | solution.py:195
  (4 shorter events, 0.0 us)
Async XLA Ops:
  1.3 14.3 %all-to-all-start = ((bf16[128,4,1]{0,2,1:T(2,128)(2,1)}), bf16[128,4,1]{0,2,1:T(2,128)(2,1)S(1)}, u32[]{:S(2)}, u32[]{:S(2)}) async-start(bf16[128,4,1]{0,2,1:T(2,128)(2,1)} %broadcast_in_dim.51), calls=%async_computation | async-start | bytes 4096 | tf_op jit(solution)/shard_map/all_to_all | solution.py:175
  8.3 6.4 %copy-start = (bf16[1,128,1024]{2,1,0:T(8,128)(2,1)S(1)}, bf16[1,128,1024]{2,1,0:T(8,128)(2,1)}, u32[]{:S(2)}) copy-start(bf16[1,128,1024]{2,1,0:T(8,128)(2,1)} %param.7) | copy-start | bytes 786436
  15.6 13.4 %all-to-all-start.1 = ((bf16[128,4,256]{0,2,1:T(8,128)(2,1)}), bf16[128,4,256]{0,2,1:T(8,128)(2,1)S(1)}, u32[]{:S(2)}, u32[]{:S(2)}) async-start(bf16[128,4,256]{0,2,1:T(8,128)(2,1)} %bitcast.8), calls=%async_computation.1 | async-start | bytes 524288 | tf_op jit(solution)/shard_map/all_to_all | solution.py:173
  29.0 10.3 %all-to-all-start.3 = ((bf16[128,4,256]{0,2,1:T(8,128)(2,1)}), bf16[128,4,256]{0,2,1:T(8,128)(2,1)S(1)}, u32[]{:S(2)}, u32[]{:S(2)}) async-start(bf16[128,4,256]{0,2,1:T(8,128)(2,1)} %bitcast.19), calls=%async_computation.3 | async-start | bytes 524288 | tf_op jit(solution)/shard_map/all_to_all | solution.py:174
  39.3 49.1 %all-to-all-start.2 = ((bf16[4,128,1,2048]{1,3,2,0:T(8,128)(2,1)}), bf16[4,128,1,2048]{1,3,2,0:T(8,128)(2,1)S(1)}, u32[]{:S(2)}, u32[]{:S(2)}) async-start(bf16[4,128,1,2048]{1,3,2,0:T(8,128)(2,1)} %pad_maximum_fusion.1), calls=%async_computation.2 | async-start | bytes 4194304 | tf_op jit(solution)/shard_map/all_to_all | solution.py:168
  178.9 25.7 %collective-permute-start = (bf16[128,8192]{0,1:T(8,128)(2,1)}, bf16[128,8192]{0,1:T(8,128)(2,1)S(1)}, u32[]{:S(2)}, u32[]{:S(2)}) collective-permute-start(bf16[128,8192]{0,1:T(8,128)(2,1)} %bitcast.75), channel_id=1, source_target_pairs={{12,0},{0,4},{4,8},{8,12},{13,1},{1,5},{5,9},{9,13},{14,2},{2,6},{... | collective-permute-start | bytes 6291464 | tf_op jit(solution)/shard_map/ppermute | solution.py:21
